TPU v7x, 256 devices: a whole 4x4x8 slice. The times are simulated.
256 devices in a mesh: child: 2 (over core), row: 4 (over x), col: 32 (over y, z).
Axes of the slice: x: 4, y: 4, z: 8, core: 2. Of those that a mesh axis runs over, the one named last changes fastest.
Arguments:
- schur_blocks: bfloat16 [2, 16384, 16384], P('child', 'row', 'col'), may hold values from -2 to 2
- child_map: int32 [2, 16384], replicated, may hold values from 0 to 24575, as said below
- round_seeds: int32 [2], replicated, may hold values from 1 to 999999
Outputs:
- leaf_bases: float32 [24576, 256], P(('row', 'child', 'col'))
- fresh_samples: float32 [24576, 256], P(('row', 'child', 'col'))
Inputs may be any that keep to these rules, and one draw needn't show every extreme that they name: For each child c and each block r < 4, the entries child_map[c, r * 4096 : (r + 1) * 4096] rise strictly, lie in parent rows [r * 6144, (r + 1) * 6144), and include both ends of that range.
All inputs are finite; a program needn't handle non-finite values.
Results may differ from a plain program's by a relative error of at most 0.0031.
Values sent between devices are 32-bit elements; how exact they have to be, the bound alone decides.
A program may use at most 64 MiB of HBM per device.

v0:
```python
import jax
import jax.numpy as jnp
from jax import lax
from jax.sharding import PartitionSpec as P

NP = 24576
K = 256


def sample_rows(seed_value, parents, sample_width):
    hashed = (
        parents[:, None] * 40503
        + lax.iota(jnp.int32, sample_width)[None, :] * 9973
        + seed_value * 2654435
    )
    hashed = hashed ^ hashed >> 15 & 131071
    hashed = hashed * 73244475
    hashed = hashed ^ hashed >> 13 & 524287
    hashed = hashed * 1274126177
    hashed = hashed ^ hashed >> 16 & 65535
    unit_value = (hashed & 16777215).astype(jnp.float32) * (1.0 / 16777216.0)
    return (unit_value - 0.5) * 3.4641016


def body(schur_blocks, child_map, round_seeds):
    child_block = schur_blocks[0]
    block_rows, block_cols = child_block.shape
    child_count = lax.axis_size("child")
    col_count = lax.axis_size("col")
    row_count_axis = lax.axis_size("row")
    child_index = lax.axis_index("child")
    row_index = lax.axis_index("row")
    col_index = lax.axis_index("col")
    child_order = child_map.shape[1]
    own_map = lax.dynamic_index_in_dim(child_map, child_index, 0, keepdims=False)
    col_ids = lax.dynamic_slice_in_dim(own_map, col_index * block_cols, block_cols)
    leaf_rows = NP // row_count_axis
    own_rows = leaf_rows // (child_count * col_count)
    leaf_base = row_index * leaf_rows

    def sketch_rows(seed_list):
        samples = jnp.concatenate(
            [sample_rows(seed_value, col_ids, K) for seed_value in seed_list], axis=1
        ).astype(jnp.bfloat16)
        return jnp.dot(child_block, samples, preferred_element_type=jnp.float32)

    def extend(partial_value):
        summed = lax.psum_scatter(partial_value, "col", scatter_dimension=0, tiled=True)
        flat_map = child_map.reshape(-1)
        wanted = (
            leaf_base
            + (child_index * col_count + col_index) * own_rows
            + lax.iota(jnp.int32, own_rows)
        )
        shard_rows = lax.all_gather(summed, ("child", "col"), axis=0, tiled=True)
        gathered_pos = lax.iota(jnp.int32, shard_rows.shape[0])
        source = (
            gathered_pos // block_rows * child_order
            + row_index * block_rows
            + gathered_pos % block_rows
        )
        parent_ids = jnp.take(flat_map, source)
        select = (wanted[:, None] == parent_ids[None, :]).astype(jnp.float32)
        return jnp.dot(select, shard_rows, precision=lax.Precision.HIGHEST)

    first_leaf = extend(sketch_rows([round_seeds[0]]))
    second_leaf = extend(sketch_rows([round_seeds[1]]))
    gram_local = jnp.dot(first_leaf.T, first_leaf, precision=lax.Precision.HIGHEST)
    gram_matrix = lax.psum(gram_local, ("child", "col")) / leaf_rows
    lower_factor = jnp.linalg.cholesky(gram_matrix)
    leaf_basis = lax.linalg.triangular_solve(
        lower_factor, first_leaf, left_side=False, lower=True, transpose_a=True
    )
    coef_local = jnp.dot(leaf_basis.T, second_leaf, precision=lax.Precision.HIGHEST)
    coefficients = lax.psum(coef_local, ("child", "col")) / leaf_rows
    fresh_samples = second_leaf - jnp.dot(leaf_basis, coefficients, precision=lax.Precision.HIGHEST)
    return (leaf_basis, fresh_samples)


def solution(mesh):
    placed = (P("child", "row", "col"), P(), P())
    return jax.shard_map(
        body,
        mesh=mesh,
        in_specs=placed,
        out_specs=(P(("row", "child", "col"), None), P(("row", "child", "col"), None)),
        check_vma=False,
    )
```

profile of v0, /device:TPU:1, one launch (start us, length us, event | category | flops | bytes accessed | tf_op | source)
XLA Modules:
  0.0 1073.4 jit_solution(4717258641060240434)
XLA Ops:
  7.2 1.3 fusion.102
  9.2 0.8 dynamic-slice_multiply_fusion
  9.9 5.7 convolution_bitcast_fusion.1
  16.3 5.7 convolution_bitcast_fusion
  22.1 217.3 %reduce-scatter.3.cloned.1.call-done = f32[128,256]{0,1:T(8,128)} async-done(((f32[4096,256]{0,1:T(8,128)}), f32[128,256]{0,1:T(8,128)}) %reduce-scatter.3.cloned.1.call-update) | async-done | bytes 131088 | tf_op jit(solution)/shard_map/reduce_scatter | solution.py:48
  239.6 226.7 %reduce-scatter.5.cloned.1.call-done = f32[128,256]{0,1:T(8,128)} async-done(((f32[4096,256]{0,1:T(8,128)}), f32[128,256]{0,1:T(8,128)}) %reduce-scatter.5.cloned.1.call-update) | async-done | bytes 131088 | tf_op jit(solution)/shard_map/reduce_scatter | solution.py:48
  466.4 45.5 %gather_fusion = s32[8192]{0:T(1024)S(1)} fusion(s32[32768]{0:T(1024)S(1)} %bitcast.52, s32[8192]{0:T(1024)S(1)} %broadcast_clamp_fusion), kind=kCustom, calls=%fused_computation.clone | custom fusion | bytes 98304 | tf_op jit(solution)/shard_map/jit(_take)/gather | solution.py:62
  512.0 45.2 %all-gather.3.cloned.1.call-done = f32[8192,256]{0,1:T(8,128)} async-done(((f32[128,256]{0,1:T(8,128)}), f32[8192,256]{0,1:T(8,128)}) %all-gather.3.cloned.1.call-update) | async-done | bytes 8388624 | tf_op jit(solution)/shard_map/all_gather | solution.py:55
  557.2 8.0 fusion.4
  565.2 1.1 fusion.103
  566.4 0.2 all-reduce.6.cloned.1.call-start
  566.6 78.4 %all-gather.5.cloned.1.call-done = f32[8192,256]{0,1:T(8,128)} async-done(((f32[128,256]{0,1:T(8,128)}), f32[8192,256]{0,1:T(8,128)}) %all-gather.5.cloned.1.call-update) | async-done | bytes 8388624 | tf_op jit(solution)/shard_map/all_gather | solution.py:55
  645.0 8.0 fusion.2
  653.1 173.0 %all-reduce.4.cloned.1.call-done = f32[256,256]{0,1:T(8,128)} async-done(((f32[256,256]{0,1:T(8,128)}), f32[256,256]{0,1:T(8,128)}) %all-reduce.4.cloned.1.call-update) | async-done | bytes 262160 | tf_op jit(solution)/shard_map/psum | solution.py:69
  826.0 1.0 broadcast_multiply_fusion
  827.1 1.0 fusion.26
  828.2 11.7 %cholesky.50 = f32[128,128]{1,0:T(8,128)S(1)} custom-call(f32[128,128]{1,0:T(8,128)S(1)} %cholesky.118), custom_call_target="Cholesky" | custom-call | tf_op jit(solution)/shard_map/jit(cholesky)/cholesky | solution.py:70
  839.9 9.8 custom-call.14
  849.7 0.2 constant_dynamic-update-slice_fusion.1
  850.0 0.3 convolution_subtract_fusion.1
  850.2 11.9 %cholesky.105 = f32[128,128]{1,0:T(8,128)S(1)} custom-call(f32[128,128]{1,0:T(8,128)S(1)} %convolution_subtract_fusion.1), custom_call_target="Cholesky" | custom-call | tf_op jit(solution)/shard_map/jit(cholesky)/cholesky | solution.py:70
  862.2 0.7 compare_reduce_fusion
  864.2 3.9 while.1
  864.2 0.6 fusion.117
  864.8 1.3 bitcast_dynamic-update-slice_fusion.2
  866.2 0.6 fusion.117
  866.8 1.3 bitcast_dynamic-update-slice_fusion.2
  868.1 19.7 %custom-call.15 = f32[2,128,128]{1,2,0:T(8,128)S(1)} custom-call(f32[2,128,128]{2,1,0:T(8,128)S(1)} %get-tuple-element.10), custom_call_target="InvertDiagBlocksLowerTriangular" | custom-call | tf_op jit(solution)/shard_map/triangular_solve | solution.py:71
  888.0 0.2 convolution_subtract_fusion.2
  888.5 1.1 fusion.104
  889.6 174.9 %all-reduce.6.cloned.1.call-done = f32[256,256]{0,1:T(8,128)} async-done(((f32[256,256]{0,1:T(8,128)}), f32[256,256]{0,1:T(8,128)}) %all-reduce.6.cloned.1.call-update) | async-done | bytes 262160 | tf_op jit(solution)/shard_map/psum | solution.py:75
  1064.6 2.0 convolution_subtract_fusion
  (34 shorter events, 1.1 us)
Async XLA Ops:
  7.2 232.3 %reduce-scatter.3.cloned.1.call-start = ((), (), s32[]{:S(2)}) async-start(), calls=%async_computation.2 | async-start | bytes 4325376 | tf_op jit(solution)/shard_map/reduce_scatter | solution.py:48
  15.7 450.6 %reduce-scatter.5.cloned.1.call-start = ((), (), s32[]{:S(2)}) async-start(), calls=%async_computation.5 | async-start | bytes 4325376 | tf_op jit(solution)/shard_map/reduce_scatter | solution.py:48
  22.1 444.3 %copy-start.1 = (s32[2,16384]{1,0:T(2,128)S(1)}, s32[2,16384]{1,0:T(2,128)}, u32[]{:S(2)}) copy-start(s32[2,16384]{1,0:T(2,128)} %param.6) | copy-start | bytes 393220
  22.1 535.1 %all-gather.3.cloned.1.call-start = ((), (), s32[]{:S(2)}) async-start(), calls=%async_computation.3 | async-start | bytes 8519680 | tf_op jit(solution)/shard_map/all_gather | solution.py:55
  239.5 405.5 %all-gather.5.cloned.1.call-start = ((), (), s32[]{:S(2)}) async-start(), calls=%async_computation.6 | async-start | bytes 8519680 | tf_op jit(solution)/shard_map/all_gather | solution.py:55
  466.3 359.8 %all-reduce.4.cloned.1.call-start = ((), (), s32[]{:S(2)}) async-start(), calls=%async_computation.4 | async-start | bytes 524288 | tf_op jit(solution)/shard_map/psum | solution.py:69
  566.4 498.2 %all-reduce.6.cloned.1.call-start = ((), (), s32[]{:S(2)}) async-start(), calls=%async_computation.7 | async-start | bytes 524288 | tf_op jit(solution)/shard_map/psum | solution.py:75
  888.5 178.0 %copy-start = (f32[96,256]{1,0:T(8,128)}, f32[96,256]{1,0:T(8,128)S(1)}, u32[]{:S(2)}) copy-start(f32[96,256]{1,0:T(8,128)S(1)} %pad_maximum_fusion) | copy-start | bytes 294916
Sparse Core Ops, SparseCore 0:
  15.8 223.6 reduce-scatter.2
  243.4 222.8 reduce-scatter.4
  468.8 88.3 all-gather.2
  559.6 85.3 all-gather.4
  648.4 177.6 all-reduce.3
  889.8 174.7 all-reduce.5
where the time goes:
time: 1070 us
  waiting for transfers between devices  916 us (86%)
  other arithmetic  56.7 us (5%)
  local copies, waits for them, and re-layouts  51 us (5%)
  matrix products  32.8 us (3%)
  between operations  16.9 us (2%)
    reduce_scatter x2, waiting for transfers between devices, extend(): lax.psum_scatter(partial_value, 'col', scatter_dimension=0, tiled=True)  444 us
    psum x1, waiting for transfers between devices, body(): coefficients = lax.psum(coef_local, ('child', 'col')) / leaf_rows  175 us
    psum x1, waiting for transfers between devices, body(): gram_matrix = lax.psum(gram_local, ('child', 'col')) / leaf_rows  173 us
    all_gather x2, waiting for transfers between devices, extend(): shard_rows = lax.all_gather(summed, ('child', 'col'), axis=0, tiled=True)  124 us
    gather x1, local copies, waits for them, and re-layouts, extend(): parent_ids = jnp.take(flat_map, source)  45.5 us
    another operation x6, other arithmetic, body(): lower_factor = jnp.linalg.cholesky(gram_matrix)  34.2 us
  transfers between devices with their start and end apart: 6, of which 6 were waited for; matrix products, arithmetic and copies ran while one was open for 6% of the time, Pallas kernels for 0%

commit v1 on v0

--- a/solution.py
+++ b/solution.py
@@ -72,7 +72,7 @@
         lower_factor, first_leaf, left_side=False, lower=True, transpose_a=True
     )
     coef_local = jnp.dot(leaf_basis.T, second_leaf, precision=lax.Precision.HIGHEST)
-    coefficients = lax.psum(coef_local, ("child", "col")) / leaf_rows
+    coefficients = jnp.sum(jax.lax.all_gather(coef_local, ("child", "col")), axis=0) / leaf_rows
     fresh_samples = second_leaf - jnp.dot(leaf_basis, coefficients, precision=lax.Precision.HIGHEST)
     return (leaf_basis, fresh_samples)
 

time: 1070 us -> 1000 us (0.935)
  waiting for transfers between devices: 916 us -> 838 us
    psum x1 -> x0, waiting for transfers between devices: 175 us -> none  [body(): coefficients = lax.psum(coef_local, ('child', 'col')) / leaf_rows]
    all_gather x0 -> x1, waiting for transfers between devices: none -> 96.9 us  [body(): jax.lax.all_gather(coef_local, ('child', 'col'))]
  transfers between devices with their start and end apart: 6 -> 6, of which waited for: 6 -> 6; matrix products, arithmetic and copies ran while one was open for 6% -> 7% of each run, Pallas kernels for 0% -> 0%
where the time goes in v1:
time: 1000 us
  waiting for transfers between devices  838 us (84%)
  other arithmetic  63.5 us (6%)
  local copies, waits for them, and re-layouts  51.1 us (5%)
  matrix products  31.8 us (3%)
  between operations  16.9 us (2%)
    reduce_scatter x2, waiting for transfers between devices, extend(): lax.psum_scatter(partial_value, 'col', scatter_dimension=0, tiled=True)  444 us
    psum x1, waiting for transfers between devices, body(): gram_matrix = lax.psum(gram_local, ('child', 'col')) / leaf_rows  173 us
    all_gather x2, waiting for transfers between devices, extend(): shard_rows = lax.all_gather(summed, ('child', 'col'), axis=0, tiled=True)  124 us
    all_gather x1, waiting for transfers between devices, body(): jax.lax.all_gather(coef_local, ('child', 'col'))  96.9 us
    gather x1, local copies, waits for them, and re-layouts, extend(): parent_ids = jnp.take(flat_map, source)  45.5 us
    another operation x6, other arithmetic, body(): lower_factor = jnp.linalg.cholesky(gram_matrix)  34.2 us
  transfers between devices with their start and end apart: 6, of which 6 were waited for; matrix products, arithmetic and copies ran while one was open for 7% of the time, Pallas kernels for 0%

profile of v1, /device:TPU:1, one launch (start us, length us, event | category | flops | bytes accessed | tf_op | source)
XLA Modules:
  0.0 1001.4 jit_solution(10515843386591329316)
XLA Ops:
  7.2 1.3 fusion.102
  9.2 0.8 dynamic-slice_multiply_fusion
  9.9 5.7 convolution_bitcast_fusion.1
  16.3 5.7 convolution_bitcast_fusion
  22.1 217.3 %reduce-scatter.3.cloned.1.call-done = f32[128,256]{0,1:T(8,128)} async-done(((f32[4096,256]{0,1:T(8,128)}), f32[128,256]{0,1:T(8,128)}) %reduce-scatter.3.cloned.1.call-update) | async-done | bytes 131088 | tf_op jit(solution)/shard_map/reduce_scatter | solution.py:48
  239.6 226.7 %reduce-scatter.5.cloned.1.call-done = f32[128,256]{0,1:T(8,128)} async-done(((f32[4096,256]{0,1:T(8,128)}), f32[128,256]{0,1:T(8,128)}) %reduce-scatter.5.cloned.1.call-update) | async-done | bytes 131088 | tf_op jit(solution)/shard_map/reduce_scatter | solution.py:48
  466.4 45.5 %gather_fusion = s32[8192]{0:T(1024)S(1)} fusion(s32[32768]{0:T(1024)S(1)} %bitcast.53, s32[8192]{0:T(1024)S(1)} %broadcast_clamp_fusion), kind=kCustom, calls=%fused_computation.clone | custom fusion | bytes 98304 | tf_op jit(solution)/shard_map/jit(_take)/gather | solution.py:62
  512.0 45.2 %all-gather.5.cloned.1.call-done = f32[8192,256]{0,1:T(8,128)} async-done(((f32[128,256]{0,1:T(8,128)}), f32[8192,256]{0,1:T(8,128)}) %all-gather.5.cloned.1.call-update) | async-done | bytes 8388624 | tf_op jit(solution)/shard_map/all_gather | solution.py:55
  557.2 8.0 fusion.4
  565.2 1.1 fusion.103
  566.4 0.2 all-gather.9.cloned.1.call-start
  566.6 78.4 %all-gather.7.cloned.1.call-done = f32[8192,256]{0,1:T(8,128)} async-done(((f32[128,256]{0,1:T(8,128)}), f32[8192,256]{0,1:T(8,128)}) %all-gather.7.cloned.1.call-update) | async-done | bytes 8388624 | tf_op jit(solution)/shard_map/all_gather | solution.py:55
  645.0 8.0 fusion.2
  653.1 173.0 %all-reduce.3.cloned.1.call-done = f32[256,256]{0,1:T(8,128)} async-done(((f32[256,256]{0,1:T(8,128)}), f32[256,256]{0,1:T(8,128)}) %all-reduce.3.cloned.1.call-update) | async-done | bytes 262160 | tf_op jit(solution)/shard_map/psum | solution.py:69
  826.0 1.0 broadcast_multiply_fusion
  827.1 1.0 fusion.26
  828.2 11.7 %cholesky.50 = f32[128,128]{1,0:T(8,128)S(1)} custom-call(f32[128,128]{1,0:T(8,128)S(1)} %cholesky.118), custom_call_target="Cholesky" | custom-call | tf_op jit(solution)/shard_map/jit(cholesky)/cholesky | solution.py:70
  839.9 9.8 custom-call.14
  850.0 0.3 convolution_subtract_fusion.1
  850.2 11.9 %cholesky.105 = f32[128,128]{1,0:T(8,128)S(1)} custom-call(f32[128,128]{1,0:T(8,128)S(1)} %convolution_subtract_fusion.1), custom_call_target="Cholesky" | custom-call | tf_op jit(solution)/shard_map/jit(cholesky)/cholesky | solution.py:70
  862.2 0.7 compare_reduce_fusion
  864.2 3.9 while.1
  864.2 0.6 fusion.117
  864.8 1.3 bitcast_dynamic-update-slice_fusion.2
  866.2 0.6 fusion.117
  866.8 1.3 bitcast_dynamic-update-slice_fusion.2
  868.1 19.7 %custom-call.15 = f32[2,128,128]{1,2,0:T(8,128)S(1)} custom-call(f32[2,128,128]{2,1,0:T(8,128)S(1)} %get-tuple-element.10), custom_call_target="InvertDiagBlocksLowerTriangular" | custom-call | tf_op jit(solution)/shard_map/triangular_solve | solution.py:71
  888.0 0.2 convolution_subtract_fusion.2
  888.5 1.1 fusion.104
  889.7 96.9 %all-gather.9.cloned.1.call-done = f32[16384,256]{1,0:T(8,128)} async-done(((f32[256,256]{1,0:T(8,128)}), f32[16384,256]{1,0:T(8,128)}) %all-gather.9.cloned.1.call-update) | async-done | bytes 16777232 | tf_op jit(solution)/shard_map/all_gather | solution.py:75
  986.5 6.8 reduce_sum.9
  993.5 1.0 convolution_subtract_fusion
  (36 shorter events, 1.4 us)
Async XLA Ops:
  7.2 232.3 %reduce-scatter.3.cloned.1.call-start = ((), (), s32[]{:S(2)}) async-start(), calls=%async_computation.2 | async-start | bytes 4325376 | tf_op jit(solution)/shard_map/reduce_scatter | solution.py:48
  15.7 450.6 %reduce-scatter.5.cloned.1.call-start = ((), (), s32[]{:S(2)}) async-start(), calls=%async_computation.5 | async-start | bytes 4325376 | tf_op jit(solution)/shard_map/reduce_scatter | solution.py:48
  22.1 444.3 %copy-start.1 = (s32[2,16384]{1,0:T(2,128)S(1)}, s32[2,16384]{1,0:T(2,128)}, u32[]{:S(2)}) copy-start(s32[2,16384]{1,0:T(2,128)} %param.6) | copy-start | bytes 393220
  22.1 535.1 %all-gather.5.cloned.1.call-start = ((), (), s32[]{:S(2)}) async-start(), calls=%async_computation.3 | async-start | bytes 8519680 | tf_op jit(solution)/shard_map/all_gather | solution.py:55
  239.5 405.5 %all-gather.7.cloned.1.call-start = ((), (), s32[]{:S(2)}) async-start(), calls=%async_computation.6 | async-start | bytes 8519680 | tf_op jit(solution)/shard_map/all_gather | solution.py:55
  466.3 359.8 %all-reduce.3.cloned.1.call-start = ((), (), s32[]{:S(2)}) async-start(), calls=%async_computation.4 | async-start | bytes 524288 | tf_op jit(solution)/shard_map/psum | solution.py:69
  566.4 420.2 %all-gather.9.cloned.1.call-start = ((), (), s32[]{:S(2)}) async-start(), calls=%async_computation.7 | async-start | bytes 17039360 | tf_op jit(solution)/shard_map/all_gather | solution.py:75
  888.5 105.0 %copy-start = (f32[96,256]{1,0:T(8,128)}, f32[96,256]{1,0:T(8,128)S(1)}, u32[]{:S(2)}) copy-start(f32[96,256]{1,0:T(8,128)S(1)} %pad_maximum_fusion) | copy-start | bytes 294916
Sparse Core Ops, SparseCore 0:
  15.8 223.6 reduce-scatter.2
  243.4 222.8 reduce-scatter.4
  468.8 88.3 all-gather.4
  559.6 85.3 all-gather.6
  648.4 177.6 all-reduce.2
  889.8 96.7 all-gather.8
